TPU v7x, 128 devices: a whole 4x4x4 slice. The times are simulated.
128 devices in a mesh: grp: 32 (over z, x_hi, y), head: 4 (over x_lo, core).
Axes of the slice: x: 4 (x_hi: 2, x_lo: 2; x = x_hi * 2 + x_lo), y: 4, z: 4, core: 2. Of those that a mesh axis runs over, the one named last changes fastest.
Arguments:
- hidden_in: bfloat16 [32, 128, 2048], P('grp'), may hold values from -6 to 6
- attn_gain: float32 [2048], replicated, may hold values from 0.1 to 1.9
- w_query: bfloat16 [2048, 2048], P(None, 'head'), may hold values from -0.125 to 0.125
- w_key: bfloat16 [2048, 2048], P(None, 'head'), may hold values from -0.125 to 0.125
- w_value: bfloat16 [2048, 2048], P(None, 'head'), may hold values from -0.125 to 0.125
- w_out: bfloat16 [2048, 2048], P('head'), may hold values from -0.125 to 0.125
- cache: bfloat16 [2, 32, 4096, 2048], P(None, None, 'grp', 'head'), may hold values from -900 to 900
- prefix_len: int32 [32], replicated, may hold values from 1 to 4096, 65536 in all
- mlp_gain: float32 [2048], replicated, may hold values from 0.1 to 1.9
- expert_ids: int32 [32, 128, 8], P('grp'), may hold values from 0 to 63, all different within a row; in each aligned block of 128 rows (0 to 127, 128 to 255, ..., all dimensions but the last counted through in order) at most 24 rows name the same one
- route_weight: float32 [32, 128, 8], P('grp'), may hold values from 0.05 to 1
- w_gate: bfloat16 [64, 2048, 1024], P('grp', None, 'head'), may hold values from -0.125 to 0.125
- w_up: bfloat16 [64, 2048, 1024], P('grp', None, 'head'), may hold values from -0.125 to 0.125
- w_down: bfloat16 [64, 1024, 2048], P('grp', 'head'), may hold values from -0.1875 to 0.1875
Outputs:
- layer_out: bfloat16 [32, 128, 2048], P('grp', None, 'head')
Inputs may be any that keep to these rules, and one draw needn't show every extreme that they name: `expert_ids`: among one prompt's 128 tokens no expert is chosen more than 24 times; a token's 8 experts are distinct.
All inputs are finite; a program needn't handle non-finite values.
Results may differ from a plain program's by a relative error of at most 0.017.
The roundings to bfloat16 on the way count: a program that leaves them out, or rounds other values in their place, can miss the bound.
Values may be sent and summed in bfloat16 or wider, within the bound.
A program may use at most 128 MiB of HBM per device.

v0:
```python
import jax
import jax.numpy as jnp
from jax import lax
from jax.sharding import PartitionSpec as P

HD = 128
TOPK = 8


def rms_norm(values, gain):
    scale = lax.rsqrt(jnp.mean(values * values, axis=-1, keepdims=True) + 1e-05)
    return values * scale * gain


def rotate(tensor, position):
    half = HD // 2
    inverse = 10000.0 ** (-(jnp.arange(half).astype(jnp.float32) * 2.0) / HD)
    angle = position[:, None] * inverse[None, :]
    cosine = jnp.cos(angle)[:, None, :]
    sine = jnp.sin(angle)[:, None, :]
    first = tensor[..., :half]
    second = tensor[..., half:]
    return jnp.concatenate(
        [first * cosine - second * sine, second * cosine + first * sine], axis=-1
    )


def on_device(
    hidden_in,
    attn_gain,
    w_query,
    w_key,
    w_value,
    w_out,
    cache,
    prefix_len,
    mlp_gain,
    expert_ids,
    route_weight,
    w_gate,
    w_up,
    w_down,
):
    group_count = lax.axis_size("grp")
    head_count = lax.axis_size("head")
    my_prompt = lax.axis_index("grp")
    tokens = hidden_in.shape[1]
    width = hidden_in.shape[2]
    heads_here = w_query.shape[1] // HD
    length = prefix_len[my_prompt]
    rows = hidden_in[0].astype(jnp.float32)
    normed = rms_norm(rows, attn_gain).astype(jnp.bfloat16)
    position = (length + jnp.arange(tokens)).astype(jnp.float32)
    query = jnp.dot(normed, w_query, preferred_element_type=jnp.float32).reshape(
        tokens, heads_here, HD
    )
    key_new = jnp.dot(normed, w_key, preferred_element_type=jnp.float32).reshape(
        tokens, heads_here, HD
    )
    value_new = jnp.dot(normed, w_value, preferred_element_type=jnp.float32).reshape(
        tokens, heads_here, HD
    )
    query = (rotate(query, position) * HD ** (-0.5)).astype(jnp.bfloat16)
    key_new = rotate(key_new, position).astype(jnp.bfloat16)
    value_new = value_new.astype(jnp.bfloat16)
    relaid = lax.all_to_all(cache, "grp", split_axis=1, concat_axis=2, tiled=True)
    context = relaid.shape[2]
    cache_key = relaid[0, 0].reshape(context, heads_here, HD)
    cache_value = relaid[1, 0].reshape(context, heads_here, HD)
    score_old = jnp.einsum("qhd,khd->hqk", query, cache_key, preferred_element_type=jnp.float32)
    score_new = jnp.einsum("qhd,khd->hqk", query, key_new, preferred_element_type=jnp.float32)
    allow_old = (jnp.arange(context) < length)[None, None, :]
    allow_new = (jnp.arange(tokens)[None, :] <= jnp.arange(tokens)[:, None])[None, :, :]
    score_old = jnp.where(allow_old, score_old, -1e30)
    score_new = jnp.where(allow_new, score_new, -1e30)
    top = jnp.maximum(
        jnp.max(score_old, axis=-1, keepdims=True), jnp.max(score_new, axis=-1, keepdims=True)
    )
    prob_old = jnp.where(allow_old, jnp.exp(score_old - top), 0.0)
    prob_new = jnp.where(allow_new, jnp.exp(score_new - top), 0.0)
    total = jnp.sum(prob_old, axis=-1) + jnp.sum(prob_new, axis=-1)
    numer = jnp.einsum(
        "hqk,khd->qhd",
        prob_old.astype(jnp.bfloat16),
        cache_value,
        preferred_element_type=jnp.float32,
    )
    numer = numer + jnp.einsum(
        "hqk,khd->qhd", prob_new.astype(jnp.bfloat16), value_new, preferred_element_type=jnp.float32
    )
    attended = (
        (numer / jnp.transpose(total)[:, :, None])
        .reshape(tokens, heads_here * HD)
        .astype(jnp.bfloat16)
    )
    projected = jnp.dot(attended, w_out, preferred_element_type=jnp.float32)
    resid = rows + lax.psum(projected.astype(jnp.bfloat16), "head").astype(jnp.float32)
    mixed_in = rms_norm(resid, mlp_gain).astype(jnp.bfloat16)
    experts_here = w_gate.shape[0]
    expert_total = experts_here * group_count
    capacity = max(2, 3 * tokens * TOPK // (2 * expert_total))
    chosen = expert_ids[0].reshape(tokens * TOPK)
    weights = route_weight[0]
    one_hot = (chosen[:, None] == jnp.arange(expert_total)[None, :]).astype(jnp.int32)
    before = jnp.cumsum(one_hot, axis=0) - one_hot
    slot = jnp.sum(before * one_hot, axis=1)
    target = chosen * capacity + slot
    repeated = jnp.repeat(mixed_in, TOPK, axis=0)
    outgoing = jnp.zeros((expert_total * capacity, width), jnp.bfloat16).at[target].set(repeated)
    outgoing = outgoing.reshape(group_count, experts_here, capacity, width)
    arrived = lax.all_to_all(outgoing, "grp", split_axis=0, concat_axis=0, tiled=True)
    results = []
    for expert in range(experts_here):
        inputs = arrived[:, expert].reshape(group_count * capacity, width)
        gate = jnp.dot(inputs, w_gate[expert], preferred_element_type=jnp.float32)
        upper = jnp.dot(inputs, w_up[expert], preferred_element_type=jnp.float32)
        act = (jax.nn.silu(gate) * upper).astype(jnp.bfloat16)
        output = jnp.dot(act, w_down[expert], preferred_element_type=jnp.float32).astype(
            jnp.bfloat16
        )
        results.append(output.reshape(group_count, capacity, width))
    expert_out = jnp.stack(results, axis=1)
    share_width = width // head_count
    returned = lax.all_to_all(expert_out, "grp", split_axis=0, concat_axis=0, tiled=True)
    returned = returned.reshape(expert_total * capacity, width)
    picked = returned[target].reshape(tokens, TOPK, width)
    combined = jnp.einsum("tk,tkd->td", weights, picked.astype(jnp.float32))
    moe_share = lax.psum_scatter(
        combined.astype(jnp.bfloat16), "head", scatter_dimension=1, tiled=True
    ).astype(jnp.float32)
    resid_share = lax.dynamic_slice_in_dim(
        resid, lax.axis_index("head") * share_width, share_width, 1
    )
    return (resid_share + moe_share).astype(jnp.bfloat16)[None]


def solution(mesh):
    placed = (
        P("grp", None, None),
        P(),
        P(None, "head"),
        P(None, "head"),
        P(None, "head"),
        P("head", None),
        P(None, None, "grp", "head"),
        P(),
        P(),
        P("grp", None, None),
        P("grp", None, None),
        P("grp", None, "head"),
        P("grp", None, "head"),
        P("grp", "head", None),
    )
    return jax.shard_map(
        on_device, mesh=mesh, in_specs=placed, out_specs=P("grp", None, "head"), check_vma=False
    )
```

profile of v0, /device:TPU:1, one launch (start us, length us, event | category | flops | bytes accessed | tf_op | source)
XLA Modules:
  0.0 487.7 jit_solution(10138498314555336373)
XLA Ops:
  6.5 0.0 copy-start
  6.5 7.7 %copy.39 = bf16[2,32,128,512]{3,2,0,1:T(8,128)(2,1)} copy(bf16[2,32,128,512]{3,2,1,0:T(8,128)(2,1)} %param.20) | data formatting | bytes 16777216 | tf_op args[6]
  14.3 11.6 %all-to-all-start = ((bf16[2,32,128,512]{3,2,0,1:T(8,128)(2,1)}), bf16[2,32,128,512]{3,2,0,1:T(8,128)(2,1)}, u32[]{:S(2)}, u32[]{:S(2)}) async-start(bf16[2,32,128,512]{3,2,0,1:T(8,128)(2,1)} %copy.39), calls=%async_computation | async-start | bytes 16777216 | tf_op jit(solution)/shard_map/all_to_all | solution.py:66
  25.9 0.0 all-reduce.2.cloned.1.call-start
  25.9 0.1 copy.51
  26.0 0.1 eq.29
  26.1 0.1 eq.25
  26.2 0.1 copy.50
  26.3 0.1 mul.196
  26.5 18.0 %reduce-window.6 = s32[64,8,128]{2,1,0:T(8,128)S(1)} reduce-window(s32[64,8,128]{2,1,0:T(8,128)S(1)} %fusion.67, s32[]{:T(128)} %constant.22.clone.1), window={size=1x1x128 pad=0_0x0_0x127_0}, to_apply=%region_6.7 | reduce-window | flops 8323072 | bytes 524292 | tf_op jit(solution)/shard_map/reduce-window
  44.5 0.1 slice.75
  44.6 0.1 copy.53
  44.8 0.1 copy.54
  44.9 4.0 copy.69
  48.9 4.0 copy.65
  52.9 4.0 copy.71
  56.9 0.6 dynamic_slice.6
  57.4 0.7 add_convert_fusion.2
  58.1 0.7 iota_compare_fusion.3
  58.8 0.2 fusion.29
  59.0 0.2 multiply_cosine_fusion
  59.2 2.4 fusion.92
  61.6 2.4 fusion.94
  64.0 0.1 subtract_convert_fusion
  64.1 0.3 fusion.98
  64.3 73.1 %all-to-all-done = bf16[2,32,128,512]{3,2,0,1:T(8,128)(2,1)} async-done(((bf16[2,32,128,512]{3,2,0,1:T(8,128)(2,1)}), bf16[2,32,128,512]{3,2,0,1:T(8,128)(2,1)}, u32[]{:S(2)}, u32[]{:S(2)}) %all-to-all-start) | async-done | bytes 8388640 | tf_op jit(solution)/shard_map/all_to_all | solution.py:66
  137.4 5.9 %fusion.96 = (bf16[1,32,128,512]{3,2,0,1:T(8,128)(2,1)}, bf16[1,32,128,512]{3,2,0,1:T(8,128)(2,1)}) fusion(bf16[2,32,128,512]{3,2,0,1:T(8,128)(2,1)} %all-to-all-done), kind=kLoop, calls=%fused_computation.121 | loop fusion | bytes 16777216 | tf_op jit(solution)/shard_map/slice | solution.py:68
  143.3 6.9 %reshape.243 = bf16[4096,4,128]{2,1,0:T(4,128)(2,1)} reshape(bf16[1,32,128,512]{3,2,0,1:T(8,128)(2,1)} %get-tuple-element.6) | data formatting | bytes 8388608 | tf_op jit(solution)/shard_map/reshape;squeeze | solution.py:69
  150.2 6.9 %reshape.242 = bf16[4096,4,128]{2,1,0:T(4,128)(2,1)} reshape(bf16[1,32,128,512]{3,2,0,1:T(8,128)(2,1)} %get-tuple-element.5) | data formatting | bytes 8388608 | tf_op jit(solution)/shard_map/reshape;squeeze | solution.py:68
  157.1 3.8 select_reduce_fusion
  161.0 2.2 fusion
  163.2 0.0 copy-done.3
  163.2 3.4 fusion.23
  166.6 0.1 fusion.68
  166.7 0.0 copy-start.8
  166.7 2.6 fusion.28
  169.3 0.0 copy-done
  169.3 1.3 convolution_convert_fusion.2
  170.6 0.0 all-reduce.2.cloned.1.call-update
  170.7 0.1 broadcast_add_fusion
  170.8 0.1 fusion.65
  170.9 52.3 %all-reduce.2.cloned.1.call-done = bf16[128,2048]{1,0:T(8,128)(2,1)} async-done(((bf16[128,2048]{1,0:T(8,128)(2,1)}), bf16[128,2048]{1,0:T(8,128)(2,1)}) %all-reduce.2.cloned.1.call-update) | async-done | bytes 524304 | tf_op jit(solution)/shard_map/psum | solution.py:97
  223.2 2.3 fusion.17
  225.4 1.3 multiply_convert_fusion
  226.7 10.4 %scatter_custom_fusion = bf16[1536,2048]{1,0:T(8,128)(2,1)} fusion(s32[1024]{0:T(1024)S(1)} %bitcast.138, bf16[]{:T(256)} %constant.49.clone.1, bf16[128,2048]{1,0:T(8,128)(2,1)S(1)} %multiply_convert_fusion), kind=kCustom, calls=%fused_computation.10 | custom fusion | bytes 6815746 | tf_op jit(solution)/shard_map/scatter | solution.py:109
  237.1 82.5 %all_to_all.19 = bf16[32,2,24,2048]{3,2,1,0:T(8,128)(2,1)S(1)} all-to-all(bf16[32,2,24,2048]{3,2,1,0:T(8,128)(2,1)} %bitcast.120), channel_id=1, replica_groups=mesh['grp'=32,'head'=4] {'grp'}, dimensions={0} | all-to-all | bytes 12582912 | tf_op jit(solution)/shard_map/all_to_all | solution.py:111
  319.6 1.1 fusion.97
  320.7 1.7 copy-done.5
  322.4 1.9 fusion.35
  324.3 1.0 fusion.40
  325.3 0.0 copy-start.11
  325.3 7.9 %convolution_convert_fusion = bf16[768,2048]{1,0:T(8,128)(2,1)} fusion(bf16[768,2048]{1,0:T(8,128)(2,1)} %bitcast.126, bf16[2,256,2048]{2,1,0:T(8,128)(2,1)} %param.27, bf16[2,2048,256]{2,1,0:T(8,128)(2,1)} %param.26, f32[768,256]{1,0:T(8,128)} %fusion.35), kind=kOutput, calls=%fused_computation.19 | convolution fusion | flops 1613365248 | bytes 9175040 | tf_op jit(solution)/shard_map/dot_general | solution.py:118
  333.2 7.1 %convolution_convert_fusion.1 = bf16[768,2048]{1,0:T(8,128)(2,1)} fusion(bf16[768,2048]{1,0:T(8,128)(2,1)} %bitcast.124, bf16[2,256,2048]{2,1,0:T(8,128)(2,1)S(1)} %copy-done.11, bf16[2,2048,256]{2,1,0:T(8,128)(2,1)} %param.26, f32[768,256]{1,0:T(8,128)S(1)} %fusion.40), kind=kOutput, calls=%fused_computation.20 | convolution fusion | flops 1613365248 | bytes 9175040 | tf_op jit(solution)/shard_map/dot_general | solution.py:118
  340.3 6.1 %pad_maximum_fusion = bf16[32,2,24,2048]{3,2,1,0:T(8,128)(2,1)} fusion(bf16[32,1,24,2048]{3,2,1,0:T(8,128)(2,1)} %bitcast.127, bf16[32,1,24,2048]{3,2,1,0:T(8,128)(2,1)} %bitcast.128), kind=kLoop, calls=%fused_computation.6 | loop fusion | flops 3145728 | bytes 12582912 | tf_op jit(solution)/shard_map/stack | solution.py:122
  346.4 7.3 %all-to-all-start.2 = ((bf16[32,2,24,2048]{3,2,1,0:T(8,128)(2,1)}), bf16[32,2,24,2048]{3,2,1,0:T(8,128)(2,1)}, u32[]{:S(2)}, u32[]{:S(2)}) async-start(bf16[32,2,24,2048]{3,2,1,0:T(8,128)(2,1)} %pad_maximum_fusion), calls=%async_computation.2 | async-start | bytes 12582912 | tf_op jit(solution)/shard_map/all_to_all | solution.py:124
  353.7 0.0 reduce-scatter.2.cloned.1.call-start
  353.8 0.1 copy.63
  354.0 87.2 %all-to-all-done.2 = bf16[32,2,24,2048]{3,2,1,0:T(8,128)(2,1)} async-done(((bf16[32,2,24,2048]{3,2,1,0:T(8,128)(2,1)}), bf16[32,2,24,2048]{3,2,1,0:T(8,128)(2,1)}, u32[]{:S(2)}, u32[]{:S(2)}) %all-to-all-start.2) | async-done | bytes 6291488 | tf_op jit(solution)/shard_map/all_to_all | solution.py:124
  441.1 12.8 %gather_fusion = bf16[1024,2048]{1,0:T(8,128)(2,1)} fusion(bf16[1536,2048]{1,0:T(8,128)(2,1)} %bitcast.32, s32[1024]{0:T(1024)S(1)} %broadcast_clamp_fusion), kind=kCustom, calls=%fused_computation | custom fusion | bytes 8392704 | tf_op jit(solution)/shard_map/gather | solution.py:126
  453.9 3.4 fusion.4
  457.3 1.1 copy.83
  458.4 0.0 reduce-scatter.2.cloned.1.call-update
  458.5 20.7 %reduce-scatter.2.cloned.1.call-done = bf16[128,512]{1,0:T(8,128)(2,1)} async-done(((bf16[128,2048]{1,0:T(8,128)(2,1)}), bf16[128,512]{1,0:T(8,128)(2,1)}) %reduce-scatter.2.cloned.1.call-update) | async-done | bytes 131088 | tf_op jit(solution)/shard_map/reduce_scatter | solution.py:128
  479.2 1.7 fusion.71
  (32 shorter events, 0.2 us)
Async XLA Ops:
  6.5 162.8 %copy-start = (bf16[512,2048]{1,0:T(8,128)(2,1)S(1)}, bf16[512,2048]{1,0:T(8,128)(2,1)}, u32[]{:S(2)}) copy-start(bf16[512,2048]{1,0:T(8,128)(2,1)} %param.19) | copy-start | bytes 6291460
  14.3 11.7 %copy-start.7 = (s32[1,128,8]{1,2,0:T(8,128)S(1)}, s32[1,128,8]{1,2,0:T(8,128)}, u32[]{:S(2)}) copy-start(s32[1,128,8]{1,2,0:T(8,128)} %param.23) | copy-start | bytes 12292
  14.3 123.1 %all-to-all-start = ((bf16[2,32,128,512]{3,2,0,1:T(8,128)(2,1)}), bf16[2,32,128,512]{3,2,0,1:T(8,128)(2,1)}, u32[]{:S(2)}, u32[]{:S(2)}) async-start(bf16[2,32,128,512]{3,2,0,1:T(8,128)(2,1)} %copy.39), calls=%async_computation | async-start | bytes 16777216 | tf_op jit(solution)/shard_map/all_to_all | solution.py:66
  25.9 197.3 %all-reduce.2.cloned.1.call-start = ((), (), s32[]{:S(2)}) async-start(), calls=%async_computation.4 | async-start | bytes 1048576 | tf_op jit(solution)/shard_map/psum | solution.py:97
  48.9 8.0 %copy-start.12 = (s32[32]{0:T(128)S(1)}, s32[32]{0:T(128)}, u32[]{:S(2)}) copy-start(s32[32]{0:T(128)} %param.21) | copy-start | bytes 388
  48.9 9.9 %copy-start.2 = (bf16[1,128,2048]{2,1,0:T(8,128)(2,1)S(1)}, bf16[1,128,2048]{2,1,0:T(8,128)(2,1)}, u32[]{:S(2)}) copy-start(bf16[1,128,2048]{2,1,0:T(8,128)(2,1)} %param.14) | copy-start | bytes 1572868
  48.9 10.4 %copy-start.6 = (f32[2048]{0:T(1024)S(1)}, f32[2048]{0:T(1024)}, u32[]{:S(2)}) copy-start(f32[2048]{0:T(1024)} %param.15) | copy-start | bytes 24580
  160.9 2.2 copy-start.3
  166.7 58.8 %copy-start.8 = (f32[2048]{0:T(1024)S(1)}, f32[2048]{0:T(1024)}, u32[]{:S(2)}) copy-start(f32[2048]{0:T(1024)} %param.22) | copy-start | bytes 24580
  319.6 2.8 copy-start.10
  320.7 1.7 copy-start.5
  320.7 3.6 copy-start.4
  325.3 7.9 %copy-start.11 = (bf16[2,256,2048]{2,1,0:T(8,128)(2,1)S(1)}, bf16[2,256,2048]{2,1,0:T(8,128)(2,1)}, u32[]{:S(2)}) copy-start(bf16[2,256,2048]{2,1,0:T(8,128)(2,1)} %param.27) | copy-start | bytes 6291460
  346.4 7.4 %copy-start.9 = (f32[1,128,8]{1,2,0:T(8,128)S(1)}, f32[1,128,8]{1,2,0:T(8,128)}, u32[]{:S(2)}) copy-start(f32[1,128,8]{1,2,0:T(8,128)} %param.24) | copy-start | bytes 12292
  346.4 94.7 %all-to-all-start.2 = ((bf16[32,2,24,2048]{3,2,1,0:T(8,128)(2,1)}), bf16[32,2,24,2048]{3,2,1,0:T(8,128)(2,1)}, u32[]{:S(2)}, u32[]{:S(2)}) async-start(bf16[32,2,24,2048]{3,2,1,0:T(8,128)(2,1)} %pad_maximum_fusion), calls=%async_computation.2 | async-start | bytes 12582912 | tf_op jit(solution)/shard_map/all_to_all | solution.py:124
  353.7 125.5 %reduce-scatter.2.cloned.1.call-start = ((), (), s32[]{:S(2)}) async-start(), calls=%async_computation.5 | async-start | bytes 655360 | tf_op jit(solution)/shard_map/reduce_scatter | solution.py:128
  441.1 39.8 %copy-start.1 = (bf16[512,2048]{1,0:T(8,128)(2,1)S(1)}, bf16[512,2048]{1,0:T(8,128)(2,1)}, u32[]{:S(2)}) copy-start(bf16[512,2048]{1,0:T(8,128)(2,1)} %param.19) | copy-start | bytes 6291460
Sparse Core Ops, SparseCore 0:
  170.8 52.3 all-reduce.1
  458.6 20.5 reduce-scatter.1
where the time goes:
time: 489 us; the launch traced here: 488 us
  waiting for transfers between devices  233 us (48%)
  blocking collectives  82.5 us (17%)
  local copies, waits for them, and re-layouts  68.1 us (14%)
  matrix products  37.4 us (8%)
  other arithmetic  33.7 us (7%)
  starting transfers between devices  19 us (4%)
  between operations  13.7 us (3%)
    all_to_all x1, waiting for transfers between devices, on_device(): lax.all_to_all(expert_out, 'grp', split_axis=0, concat_axis=0, tiled=True)  87.2 us
    all_to_all x1, blocking collectives, on_device(): lax.all_to_all(outgoing, 'grp', split_axis=0, concat_axis=0, tiled=True)  82.5 us
    all_to_all x1, waiting for transfers between devices, on_device(): lax.all_to_all(cache, 'grp', split_axis=1, concat_axis=2, tiled=True)  73.1 us
    psum x1, waiting for transfers between devices, on_device(): lax.psum(projected.astype(jnp.bfloat16), 'head').astype(jnp.float32)  52.3 us
    reduce_scatter x1, waiting for transfers between devices, on_device(): lax.psum_scatter(combined.astype(jnp.bfloat16), 'head', scatter_dimension...  20.7 us
    another operation x4, other arithmetic  18.2 us
    dot_general x2, matrix products, on_device(): jnp.dot(act, w_down[expert], preferred_element_type=jnp.float32)  15 us
    gather x1, local copies, waits for them, and re-layouts, on_device(): picked = returned[target].reshape(tokens, TOPK, width)  12.8 us
  transfers between devices with their start and end apart: 4, of which 4 were waited for; matrix products, arithmetic and copies ran while one was open for 8% of the time, Pallas kernels for 0%

commit v1 on v0

--- a/solution.py
+++ b/solution.py
@@ -2,6 +2,7 @@
 import jax.numpy as jnp
 from jax import lax
 from jax.sharding import PartitionSpec as P
+from jax.lax import all_gather
 
 HD = 128
 TOPK = 8
@@ -94,7 +95,12 @@
         .astype(jnp.bfloat16)
     )
     projected = jnp.dot(attended, w_out, preferred_element_type=jnp.float32)
-    resid = rows + lax.psum(projected.astype(jnp.bfloat16), "head").astype(jnp.float32)
+
+    def _do_surface(x_part):
+        local_part = all_gather(x_part, axis_name="head")
+        return jnp.sum(local_part, axis=0)
+
+    resid = rows + _do_surface(projected.astype(jnp.bfloat16)).astype(jnp.float32)
     mixed_in = rms_norm(resid, mlp_gain).astype(jnp.bfloat16)
     experts_here = w_gate.shape[0]
     expert_total = experts_here * group_count

time: 489 us -> 478 us (0.978)
  waiting for transfers between devices: 233 us -> 224 us
    psum x1 -> x0, waiting for transfers between devices: 52.3 us -> none  [on_device(): lax.psum(projected.astype(jnp.bfloat16), 'head').astype(jnp.float32)]
    all_gather x0 -> x1, waiting for transfers between devices: none -> 24.8 us  [_do_surface(): local_part = all_gather(x_part, axis_name='head')]
    all_to_all x1, waiting for transfers between devices: 73.1 us -> 92 us  [on_device(): lax.all_to_all(cache, 'grp', split_axis=1, concat_axis=2, tiled=True)]
where the time goes in v1:
time: 478 us; the launch traced here: 477 us
  waiting for transfers between devices  224 us (47%)
  blocking collectives  82.6 us (17%)
  local copies, waits for them, and re-layouts  68.1 us (14%)
  matrix products  35.5 us (7%)
  other arithmetic  33.6 us (7%)
  starting transfers between devices  19 us (4%)
  between operations  13.7 us (3%)
    all_to_all x1, waiting for transfers between devices, on_device(): lax.all_to_all(cache, 'grp', split_axis=1, concat_axis=2, tiled=True)  92 us
    all_to_all x1, waiting for transfers between devices, on_device(): lax.all_to_all(expert_out, 'grp', split_axis=0, concat_axis=0, tiled=True)  83.2 us
    all_to_all x1, blocking collectives, on_device(): lax.all_to_all(outgoing, 'grp', split_axis=0, concat_axis=0, tiled=True)  82.6 us
    all_gather x1, waiting for transfers between devices, _do_surface(): local_part = all_gather(x_part, axis_name='head')  24.8 us
    reduce_scatter x1, waiting for transfers between devices, on_device(): lax.psum_scatter(combined.astype(jnp.bfloat16), 'head', scatter_dimension...  24.1 us
    another operation x4, other arithmetic  18.2 us
    dot_general x2, matrix products, on_device(): jnp.dot(act, w_down[expert], preferred_element_type=jnp.float32)  15 us
    gather x1, local copies, waits for them, and re-layouts, on_device(): picked = returned[target].reshape(tokens, TOPK, width)  12.8 us
  transfers between devices with their start and end apart: 4, of which 4 were waited for; matrix products, arithmetic and copies ran while one was open for 8% of the time, Pallas kernels for 0%

profile of v1, /device:TPU:1, one launch (start us, length us, event | category | flops | bytes accessed | tf_op | source)
XLA Modules:
  0.0 476.7 jit_solution(10455435979040509885)
XLA Ops:
  6.5 0.0 copy-start
  6.5 7.7 %copy.39 = bf16[2,32,128,512]{3,2,0,1:T(8,128)(2,1)} copy(bf16[2,32,128,512]{3,2,1,0:T(8,128)(2,1)} %param.20) | data formatting | bytes 16777216 | tf_op args[6]
  14.3 11.5 %all-to-all-start = ((bf16[2,32,128,512]{3,2,0,1:T(8,128)(2,1)}), bf16[2,32,128,512]{3,2,0,1:T(8,128)(2,1)}, u32[]{:S(2)}, u32[]{:S(2)}) async-start(bf16[2,32,128,512]{3,2,0,1:T(8,128)(2,1)} %copy.39), calls=%async_computation | async-start | bytes 16777216 | tf_op jit(solution)/shard_map/all_to_all | solution.py:67
  25.8 0.0 all-gather.3.cloned.1.call-start
  25.8 4.0 copy.69
  29.8 4.0 copy.65
  33.8 4.0 copy.71
  37.8 0.6 dynamic_slice.6
  38.4 0.7 add_convert_fusion.2
  39.0 0.7 iota_compare_fusion.3
  39.7 0.2 fusion.29
  39.9 0.2 multiply_cosine_fusion
  40.1 2.4 fusion.92
  42.5 2.4 fusion.94
  44.9 0.1 subtract_convert_fusion
  45.0 0.3 fusion.98
  45.2 92.0 %all-to-all-done = bf16[2,32,128,512]{3,2,0,1:T(8,128)(2,1)} async-done(((bf16[2,32,128,512]{3,2,0,1:T(8,128)(2,1)}), bf16[2,32,128,512]{3,2,0,1:T(8,128)(2,1)}, u32[]{:S(2)}, u32[]{:S(2)}) %all-to-all-start) | async-done | bytes 8388640 | tf_op jit(solution)/shard_map/all_to_all | solution.py:67
  137.3 5.9 %fusion.96 = (bf16[1,32,128,512]{3,2,0,1:T(8,128)(2,1)}, bf16[1,32,128,512]{3,2,0,1:T(8,128)(2,1)}) fusion(bf16[2,32,128,512]{3,2,0,1:T(8,128)(2,1)} %all-to-all-done), kind=kLoop, calls=%fused_computation.121 | loop fusion | bytes 16777216 | tf_op jit(solution)/shard_map/slice | solution.py:69
  143.2 6.9 %reshape.244 = bf16[4096,4,128]{2,1,0:T(4,128)(2,1)} reshape(bf16[1,32,128,512]{3,2,0,1:T(8,128)(2,1)} %get-tuple-element.6) | data formatting | bytes 8388608 | tf_op jit(solution)/shard_map/reshape;squeeze | solution.py:70
  150.1 6.9 %reshape.243 = bf16[4096,4,128]{2,1,0:T(4,128)(2,1)} reshape(bf16[1,32,128,512]{3,2,0,1:T(8,128)(2,1)} %get-tuple-element.5) | data formatting | bytes 8388608 | tf_op jit(solution)/shard_map/reshape;squeeze | solution.py:69
  157.0 3.8 select_reduce_fusion
  160.8 2.2 fusion
  163.0 2.4 fusion.23
  165.5 0.0 copy-start.7
  165.5 0.1 fusion.68
  165.6 2.6 fusion.28
  168.2 1.3 convolution_convert_fusion.2
  169.5 0.0 all-gather.3.cloned.1.call-update
  169.5 0.1 copy.51
  169.6 0.1 eq.29
  169.7 0.1 eq.25
  169.8 0.1 copy.50
  169.9 0.1 mul.196
  170.0 18.0 %reduce-window.6 = s32[64,8,128]{2,1,0:T(8,128)S(1)} reduce-window(s32[64,8,128]{2,1,0:T(8,128)S(1)} %fusion.67, s32[]{:T(128)} %constant.22.clone.1), window={size=1x1x128 pad=0_0x0_0x127_0}, to_apply=%region_6.7 | reduce-window | flops 8323072 | bytes 524292 | tf_op jit(solution)/shard_map/reduce-window
  188.1 0.1 slice.75
  188.2 0.1 copy.53
  188.4 0.1 copy.54
  188.5 0.1 broadcast_add_fusion
  188.6 0.1 fusion.65
  188.7 24.8 %all-gather.3.cloned.1.call-done = bf16[512,2048]{1,0:T(8,128)(2,1)} async-done(((bf16[128,2048]{1,0:T(8,128)(2,1)}), bf16[512,2048]{1,0:T(8,128)(2,1)}) %all-gather.3.cloned.1.call-update) | async-done | bytes 2097168 | tf_op jit(solution)/shard_map/all_gather | solution.py:100
  213.5 2.0 reduce_sum.62
  215.5 1.2 fusion.17
  216.8 0.0 copy-done.8
  216.8 0.2 multiply_convert_fusion
  217.0 10.4 %scatter_custom_fusion = bf16[1536,2048]{1,0:T(8,128)(2,1)} fusion(s32[1024]{0:T(1024)S(1)} %bitcast.140, bf16[]{:T(256)} %constant.47.clone.1, bf16[128,2048]{1,0:T(8,128)(2,1)S(1)} %multiply_convert_fusion), kind=kCustom, calls=%fused_computation.10 | custom fusion | bytes 6815746 | tf_op jit(solution)/shard_map/scatter | solution.py:115
  227.4 82.6 %all_to_all.19 = bf16[32,2,24,2048]{3,2,1,0:T(8,128)(2,1)S(1)} all-to-all(bf16[32,2,24,2048]{3,2,1,0:T(8,128)(2,1)} %bitcast.121), channel_id=1, replica_groups=mesh['grp'=32,'head'=4] {'grp'}, dimensions={0} | all-to-all | bytes 12582912 | tf_op jit(solution)/shard_map/all_to_all | solution.py:117
  310.0 1.1 fusion.97
  311.1 0.0 copy-start.5
  311.1 1.7 copy-done.5
  312.8 1.0 fusion.35
  313.8 1.0 fusion.40
  314.8 7.5 %convolution_convert_fusion = bf16[768,2048]{1,0:T(8,128)(2,1)} fusion(bf16[768,2048]{1,0:T(8,128)(2,1)} %bitcast.127, bf16[2,256,2048]{2,1,0:T(8,128)(2,1)} %param.27, bf16[2,2048,256]{2,1,0:T(8,128)(2,1)} %param.26, f32[768,256]{1,0:T(8,128)S(1)} %fusion.35), kind=kOutput, calls=%fused_computation.19 | convolution fusion | flops 1613365248 | bytes 9175040 | tf_op jit(solution)/shard_map/dot_general | solution.py:124
  322.3 7.4 %convolution_convert_fusion.1 = bf16[768,2048]{1,0:T(8,128)(2,1)} fusion(bf16[768,2048]{1,0:T(8,128)(2,1)} %bitcast.125, bf16[2,256,2048]{2,1,0:T(8,128)(2,1)} %param.27, bf16[2,2048,256]{2,1,0:T(8,128)(2,1)} %param.26, f32[768,256]{1,0:T(8,128)S(1)} %fusion.40), kind=kOutput, calls=%fused_computation.20 | convolution fusion | flops 1613365248 | bytes 9175040 | tf_op jit(solution)/shard_map/dot_general | solution.py:124
  329.8 6.1 %pad_maximum_fusion = bf16[32,2,24,2048]{3,2,1,0:T(8,128)(2,1)} fusion(bf16[32,1,24,2048]{3,2,1,0:T(8,128)(2,1)} %bitcast.128, bf16[32,1,24,2048]{3,2,1,0:T(8,128)(2,1)} %bitcast.129), kind=kLoop, calls=%fused_computation.6 | loop fusion | flops 3145728 | bytes 12582912 | tf_op jit(solution)/shard_map/stack | solution.py:128
  335.9 7.5 %all-to-all-start.2 = ((bf16[32,2,24,2048]{3,2,1,0:T(8,128)(2,1)}), bf16[32,2,24,2048]{3,2,1,0:T(8,128)(2,1)}, u32[]{:S(2)}, u32[]{:S(2)}) async-start(bf16[32,2,24,2048]{3,2,1,0:T(8,128)(2,1)} %pad_maximum_fusion), calls=%async_computation.2 | async-start | bytes 12582912 | tf_op jit(solution)/shard_map/all_to_all | solution.py:130
  343.3 0.0 reduce-scatter.2.cloned.1.call-start
  343.4 0.1 copy.63
  343.6 83.2 %all-to-all-done.2 = bf16[32,2,24,2048]{3,2,1,0:T(8,128)(2,1)} async-done(((bf16[32,2,24,2048]{3,2,1,0:T(8,128)(2,1)}), bf16[32,2,24,2048]{3,2,1,0:T(8,128)(2,1)}, u32[]{:S(2)}, u32[]{:S(2)}) %all-to-all-start.2) | async-done | bytes 6291488 | tf_op jit(solution)/shard_map/all_to_all | solution.py:130
  426.7 12.8 %gather_fusion = bf16[1024,2048]{1,0:T(8,128)(2,1)} fusion(bf16[1536,2048]{1,0:T(8,128)(2,1)} %bitcast.33, s32[1024]{0:T(1024)S(1)} %broadcast_clamp_fusion), kind=kCustom, calls=%fused_computation | custom fusion | bytes 8392704 | tf_op jit(solution)/shard_map/gather | solution.py:132
  439.5 3.4 fusion.4
  442.9 1.1 copy.83
  444.0 0.0 reduce-scatter.2.cloned.1.call-update
  444.1 24.1 %reduce-scatter.2.cloned.1.call-done = bf16[128,512]{1,0:T(8,128)(2,1)} async-done(((bf16[128,2048]{1,0:T(8,128)(2,1)}), bf16[128,512]{1,0:T(8,128)(2,1)}) %reduce-scatter.2.cloned.1.call-update) | async-done | bytes 131088 | tf_op jit(solution)/shard_map/reduce_scatter | solution.py:134
  468.1 1.7 fusion.71
  (31 shorter events, 0.2 us)
Async XLA Ops:
  6.5 161.7 %copy-start = (bf16[512,2048]{1,0:T(8,128)(2,1)S(1)}, bf16[512,2048]{1,0:T(8,128)(2,1)}, u32[]{:S(2)}) copy-start(bf16[512,2048]{1,0:T(8,128)(2,1)} %param.19) | copy-start | bytes 6291460
  14.3 123.0 %all-to-all-start = ((bf16[2,32,128,512]{3,2,0,1:T(8,128)(2,1)}), bf16[2,32,128,512]{3,2,0,1:T(8,128)(2,1)}, u32[]{:S(2)}, u32[]{:S(2)}) async-start(bf16[2,32,128,512]{3,2,0,1:T(8,128)(2,1)} %copy.39), calls=%async_computation | async-start | bytes 16777216 | tf_op jit(solution)/shard_map/all_to_all | solution.py:67
  25.8 187.8 %all-gather.3.cloned.1.call-start = ((), (), s32[]{:S(2)}) async-start(), calls=%async_computation.5 | async-start | bytes 2621440 | tf_op jit(solution)/shard_map/all_gather | solution.py:100
  29.8 8.0 %copy-start.11 = (s32[32]{0:T(128)S(1)}, s32[32]{0:T(128)}, u32[]{:S(2)}) copy-start(s32[32]{0:T(128)} %param.21) | copy-start | bytes 388
  29.8 9.9 %copy-start.2 = (bf16[1,128,2048]{2,1,0:T(8,128)(2,1)S(1)}, bf16[1,128,2048]{2,1,0:T(8,128)(2,1)}, u32[]{:S(2)}) copy-start(bf16[1,128,2048]{2,1,0:T(8,128)(2,1)} %param.14) | copy-start | bytes 1572868
  29.8 10.4 %copy-start.6 = (f32[2048]{0:T(1024)S(1)}, f32[2048]{0:T(1024)}, u32[]{:S(2)}) copy-start(f32[2048]{0:T(1024)} %param.15) | copy-start | bytes 24580
  160.8 2.2 copy-start.3
  165.5 4.1 copy-start.7
  169.5 47.3 %copy-start.8 = (f32[2048]{0:T(1024)S(1)}, f32[2048]{0:T(1024)}, u32[]{:S(2)}) copy-start(f32[2048]{0:T(1024)} %param.22) | copy-start | bytes 24580
  310.0 2.8 copy-start.10
  311.1 1.7 copy-start.5
  311.1 2.7 copy-start.4
  335.9 7.5 %copy-start.9 = (f32[1,128,8]{1,2,0:T(8,128)S(1)}, f32[1,128,8]{1,2,0:T(8,128)}, u32[]{:S(2)}) copy-start(f32[1,128,8]{1,2,0:T(8,128)} %param.24) | copy-start | bytes 12292
  335.9 90.8 %all-to-all-start.2 = ((bf16[32,2,24,2048]{3,2,1,0:T(8,128)(2,1)}), bf16[32,2,24,2048]{3,2,1,0:T(8,128)(2,1)}, u32[]{:S(2)}, u32[]{:S(2)}) async-start(bf16[32,2,24,2048]{3,2,1,0:T(8,128)(2,1)} %pad_maximum_fusion), calls=%async_computation.2 | async-start | bytes 12582912 | tf_op jit(solution)/shard_map/all_to_all | solution.py:130
  343.3 124.8 %reduce-scatter.2.cloned.1.call-start = ((), (), s32[]{:S(2)}) async-start(), calls=%async_computation.4 | async-start | bytes 655360 | tf_op jit(solution)/shard_map/reduce_scatter | solution.py:134
  426.7 43.1 %copy-start.1 = (bf16[512,2048]{1,0:T(8,128)(2,1)S(1)}, bf16[512,2048]{1,0:T(8,128)(2,1)}, u32[]{:S(2)}) copy-start(bf16[512,2048]{1,0:T(8,128)(2,1)} %param.19) | copy-start | bytes 6291460
Sparse Core Ops, SparseCore 0:
  169.6 43.8 all-gather.2
  444.2 23.9 reduce-scatter.1
